TPU v7x, 32 devices: a whole 2x2x4 slice. The times are simulated.
32 devices in a mesh: rows: 4 (over y, x), mp: 8 (over z, core).
Axes of the slice: x: 2, y: 2, z: 4, core: 2. Of those that a mesh axis runs over, the one named last changes fastest.
Arguments:
- inputs: bfloat16 [8192, 2048], P(('rows', 'mp')), may hold values from -6 to 6
- cotangent: bfloat16 [8192, 2048], P(('rows', 'mp')), may hold values from -6 to 6
- corpus_ids: int32 [4], P('rows'), may hold values from 0 to 3
- corpus_weight: float32 [4], replicated, may hold values from 0.5 to 2
- attn_gain: bfloat16 [2048], P(('rows', 'mp')), may hold values from 0.099609375 to 1.8984375
- qkv_weight: bfloat16 [2048, 1920], P(('rows', 'mp')), may hold values from -0.125 to 0.125
- out_weight: bfloat16 [1280, 2048], P(('rows', 'mp')), may hold values from -2.5 to 2.5
- ffn_gain: bfloat16 [2048], P(('rows', 'mp')), may hold values from 0.099609375 to 1.8984375
- gate_weight: bfloat16 [2048, 6144], P(None, 'mp'), may hold values from -0.125 to 0.125
- up_weight: bfloat16 [2048, 6144], P(None, 'mp'), may hold values from -0.125 to 0.125
- down_weight: bfloat16 [6144, 2048], P('mp'), may hold values from -0.078125 to 0.078125
Outputs:
- outputs: bfloat16 [8192, 2048], P(('rows', 'mp'))
- input_grad: float32 [8192, 2048], P(('rows', 'mp'))
- qkv_grad: float32 [2048, 1920], P(('rows', 'mp'))
- proj_grad: float32 [1280, 2048], P(('rows', 'mp'))
- gate_grad: float32 [2048, 6144], P(None, 'mp')
- up_grad: float32 [2048, 6144], P(None, 'mp')
- down_grad: float32 [6144, 2048], P('mp')
- attn_gain_grad: float32 [2048], P(('rows', 'mp'))
- ffn_gain_grad: float32 [2048], P(('rows', 'mp'))
All inputs are finite; a program needn't handle non-finite values.
Results may differ from a plain program's by a relative error of at most 0.015.
Values may be sent and summed in bfloat16 or wider, within the bound.
A program may use at most 256 MiB of HBM per device.

v0:
```python
import jax
import jax.numpy as jnp
from jax import lax
from jax.sharding import PartitionSpec as P

HEADS = 20
KV_HEADS = 5
HEAD_DIM = 64
LEN = 2048
QBLOCK = 512
QBLOCKS = 4
EPS = 1e-05
THETA = 10000.0


def rotation(positions):
    half_dim = HEAD_DIM // 2
    freqs = jnp.exp(-jnp.log(THETA) * (2.0 * jnp.arange(half_dim, dtype=jnp.float32)) / HEAD_DIM)
    angles = positions.astype(jnp.float32)[:, None] * freqs[None, :]
    return (jnp.cos(angles), jnp.sin(angles))


def rotate(values_in, cosine, sine_part):
    half_dim = HEAD_DIM // 2
    first = values_in[..., :half_dim]
    second = values_in[..., half_dim:]
    return jnp.concatenate(
        [first * cosine - second * sine_part, second * cosine + first * sine_part], axis=-1
    )


def rotate_back(values_in, cosine, sine_part):
    half_dim = HEAD_DIM // 2
    first = values_in[..., :half_dim]
    second = values_in[..., half_dim:]
    return jnp.concatenate(
        [first * cosine + second * sine_part, second * cosine - first * sine_part], axis=-1
    )


def project_kv(normed, weight_kv, positions):
    row_count = normed.shape[0]
    kv_width = KV_HEADS * HEAD_DIM
    kv_raw = jnp.dot(normed, weight_kv, preferred_element_type=jnp.float32)
    cosine, sine_part = rotation(positions)
    keys_part = rotate(
        kv_raw[:, :kv_width].reshape(row_count, KV_HEADS, HEAD_DIM),
        cosine[:, None, :],
        sine_part[:, None, :],
    )
    return jnp.concatenate(
        [keys_part.reshape(row_count, kv_width), kv_raw[:, kv_width:]], axis=1
    ).astype(jnp.bfloat16)


def key_slices(kv_all, seq_start, kv_head, length):
    keys_part = lax.dynamic_slice(kv_all, (seq_start, kv_head * HEAD_DIM), (length, HEAD_DIM))
    values_part = lax.dynamic_slice(
        kv_all, (seq_start, (KV_HEADS + kv_head) * HEAD_DIM), (length, HEAD_DIM)
    )
    return (keys_part, values_part)


def masked_scores(queries, keys_part, block_index, length):
    scores = jnp.einsum(
        "qd,kd->qk", queries, keys_part, preferred_element_type=jnp.float32
    ) * HEAD_DIM ** (-0.5)
    allowed = jnp.arange(length)[None, :] <= block_index * QBLOCK + jnp.arange(QBLOCK)[:, None]
    return jnp.where(allowed, scores, -1e30)


def forward_branch(block_index):
    length = (block_index + 1) * QBLOCK

    def branch(queries, kv_all, seq_start, kv_head):
        keys_part, values_part = key_slices(kv_all, seq_start, kv_head, length)
        scores = masked_scores(queries, keys_part, block_index, length)
        row_max = jnp.max(scores, axis=1, keepdims=True)
        exponent = jnp.exp(scores - row_max)
        row_total = jnp.sum(exponent, axis=1, keepdims=True)
        probabilities = (exponent / row_total).astype(jnp.bfloat16)
        output = jnp.dot(probabilities, values_part, preferred_element_type=jnp.float32).astype(
            jnp.bfloat16
        )
        return (output, (row_max + jnp.log(row_total))[:, 0])

    return branch


def backward_branch(block_index):
    length = (block_index + 1) * QBLOCK

    def branch(queries, grad_output, log_total, kv_all, seq_start, kv_head):
        keys_part, values_part = key_slices(kv_all, seq_start, kv_head, length)
        scores = masked_scores(queries, keys_part, block_index, length)
        probabilities = jnp.exp(scores - log_total[:, None])
        grad_probs = jnp.einsum(
            "qd,kd->qk", grad_output, values_part, preferred_element_type=jnp.float32
        )
        row_delta = jnp.sum(probabilities * grad_probs, axis=1, keepdims=True)
        grad_scores = (probabilities * (grad_probs - row_delta)).astype(jnp.bfloat16)
        grad_queries = jnp.dot(
            grad_scores, keys_part, preferred_element_type=jnp.float32
        ) * HEAD_DIM ** (-0.5)
        grad_keys = jnp.einsum(
            "qk,qd->kd", grad_scores, queries, preferred_element_type=jnp.float32
        ) * HEAD_DIM ** (-0.5)
        grad_values = jnp.einsum(
            "qk,qd->kd",
            probabilities.astype(jnp.bfloat16),
            grad_output,
            preferred_element_type=jnp.float32,
        )
        padding = ((0, LEN - length), (0, 0))
        return (grad_queries, jnp.pad(grad_keys, padding), jnp.pad(grad_values, padding))

    return branch


def add_window(target, update, start_row, start_col):
    current = lax.dynamic_slice(target, (start_row, start_col), update.shape)
    return lax.dynamic_update_slice(target, current + update, (start_row, start_col))


def on_device(
    inputs,
    cotangent,
    corpus_ids,
    corpus_weight,
    attn_gain,
    qkv_weight,
    out_weight,
    ffn_gain,
    gate_weight,
    up_weight,
    down_weight,
):
    tok_dev = inputs.shape[0]
    group_rows = tok_dev * lax.axis_size("mp")
    offset = lax.axis_index("mp") * tok_dev
    seq_group = corpus_ids.shape[0]
    corpora_count = corpus_weight.shape[0]
    sequences_all = seq_group * lax.axis_size("rows")
    q_width = HEADS * HEAD_DIM
    kv_width = KV_HEADS * HEAD_DIM
    group_size = HEADS // KV_HEADS
    model_width = inputs.shape[1]
    tiles_dev = HEADS * QBLOCKS // lax.axis_size("mp")
    first_tile = lax.axis_index("mp") * tiles_dev
    chosen = (corpus_ids[:, None] == jnp.arange(corpora_count)[None, :]).astype(jnp.float32)
    counts = lax.psum(jnp.sum(chosen, axis=0), "rows")
    count_seq = jnp.sum(chosen * counts[None, :], axis=1)
    weight_seq = jnp.sum(chosen * corpus_weight[None, :], axis=1)
    seq_scale = weight_seq * sequences_all / (corpora_count * count_seq)
    qkv_full, out_full, gain_one, gain_two = (
        lax.all_gather(qkv_weight, ("rows", "mp"), axis=0, tiled=True),
        lax.all_gather(out_weight, ("rows", "mp"), axis=0, tiled=True),
        lax.all_gather(attn_gain, ("rows", "mp"), axis=0, tiled=True),
        lax.all_gather(ffn_gain, ("rows", "mp"), axis=0, tiled=True),
    )
    gain_one = gain_one.astype(jnp.float32)
    gain_two = gain_two.astype(jnp.float32)
    weight_kv = qkv_full[:, q_width:]
    residual = inputs.astype(jnp.float32)
    inverse_one = lax.rsqrt(jnp.mean(residual * residual, axis=-1, keepdims=True) + EPS)
    normed_one = (residual * inverse_one * gain_one).astype(jnp.bfloat16)
    local_pos = (offset + jnp.arange(tok_dev)) % LEN
    normed_all, kv_all = (
        lax.all_gather(normed_one, "mp", axis=0, tiled=True),
        lax.all_gather(project_kv(normed_one, weight_kv, local_pos), "mp", axis=0, tiled=True),
    )
    count_items = tiles_dev * seq_group
    forward_list = [forward_branch(b) for b in range(QBLOCKS)]
    backward_list = [backward_branch(b) for b in range(QBLOCKS)]

    def item_info(item_index):
        tile_index = first_tile + item_index // seq_group
        seq_start = item_index % seq_group * LEN
        head_index = tile_index // QBLOCKS
        block_index = tile_index % QBLOCKS
        return (head_index, block_index, seq_start, seq_start + block_index * QBLOCK)

    def forward_item(partial_value, item_index):
        head_index, block_index, seq_start, row_start = item_info(item_index)
        rows_in = lax.dynamic_slice(normed_all, (row_start, 0), (QBLOCK, model_width))
        weight_q = lax.dynamic_slice(qkv_full, (0, head_index * HEAD_DIM), (model_width, HEAD_DIM))
        raw_queries = jnp.dot(rows_in, weight_q, preferred_element_type=jnp.float32)
        cosine, sine_part = rotation(block_index * QBLOCK + jnp.arange(QBLOCK))
        queries = rotate(raw_queries, cosine, sine_part).astype(jnp.bfloat16)
        output, log_total = lax.switch(
            block_index, forward_list, queries, kv_all, seq_start, head_index // group_size
        )
        weight_o = lax.dynamic_slice(out_full, (head_index * HEAD_DIM, 0), (HEAD_DIM, model_width))
        partial_value = add_window(
            partial_value,
            jnp.dot(output, weight_o, preferred_element_type=jnp.float32),
            row_start,
            0,
        )
        return (partial_value, (queries, output, log_total))

    attn_partial, (kept_queries, kept_outputs, kept_totals) = lax.scan(
        forward_item, jnp.zeros((group_rows, model_width), jnp.float32), jnp.arange(count_items)
    )
    attn_sum = lax.psum_scatter(attn_partial, "mp", scatter_dimension=0, tiled=True)
    middle = residual + attn_sum
    inverse_two = lax.rsqrt(jnp.mean(middle * middle, axis=-1, keepdims=True) + EPS)
    normed_two = (middle * inverse_two * gain_two).astype(jnp.bfloat16)
    normed_mid = lax.all_gather(normed_two, "mp", axis=0, tiled=True)
    gate_val = jnp.dot(normed_mid, gate_weight, preferred_element_type=jnp.float32)
    up_val = jnp.dot(normed_mid, up_weight, preferred_element_type=jnp.float32)
    hidden = (jax.nn.silu(gate_val) * up_val).astype(jnp.bfloat16)
    ffn_part = jnp.dot(hidden, down_weight, preferred_element_type=jnp.float32)
    ffn_sum = lax.psum_scatter(
        ffn_part.astype(jnp.bfloat16), "mp", scatter_dimension=0, tiled=True
    ).astype(jnp.float32)
    outputs = (middle + ffn_sum).astype(jnp.bfloat16)
    seq_local = (offset + jnp.arange(tok_dev)) // LEN
    token_scale = jnp.sum(
        (seq_local[:, None] == jnp.arange(seq_group)[None, :]).astype(jnp.float32)
        * seq_scale[None, :],
        axis=1,
    )
    grad_out = cotangent.astype(jnp.float32) * token_scale[:, None]
    grad_all = lax.all_gather(grad_out.astype(jnp.bfloat16), "mp", axis=0, tiled=True)
    grad_hidden = jnp.einsum("td,fd->tf", grad_all, down_weight, preferred_element_type=jnp.float32)
    down_grad = jnp.einsum("tf,td->fd", hidden, grad_all, preferred_element_type=jnp.float32)
    sigmoid_val = jax.nn.sigmoid(gate_val)
    grad_gate = (
        grad_hidden * up_val * (sigmoid_val * (1.0 + gate_val * (1.0 - sigmoid_val)))
    ).astype(jnp.bfloat16)
    grad_up = (grad_hidden * (gate_val * sigmoid_val)).astype(jnp.bfloat16)
    gate_grad = jnp.einsum("td,tf->df", normed_mid, grad_gate, preferred_element_type=jnp.float32)
    up_grad = jnp.einsum("td,tf->df", normed_mid, grad_up, preferred_element_type=jnp.float32)
    mid_partial = jnp.einsum(
        "tf,df->td", grad_gate, gate_weight, preferred_element_type=jnp.float32
    )
    mid_partial = mid_partial + jnp.einsum(
        "tf,df->td", grad_up, up_weight, preferred_element_type=jnp.float32
    )
    grad_normed_two = lax.psum_scatter(mid_partial, "mp", scatter_dimension=0, tiled=True)
    scaled_two = grad_normed_two * gain_two
    ffn_gain_part = jnp.sum(grad_normed_two * middle * inverse_two, axis=0)
    grad_middle = (
        grad_out
        + inverse_two * scaled_two
        - middle * inverse_two**3 * jnp.mean(scaled_two * middle, axis=-1, keepdims=True)
    )
    grad_attn_all = lax.all_gather(grad_middle.astype(jnp.bfloat16), "mp", axis=0, tiled=True)

    def backward_item(carried, item_index):
        input_partial, kv_partial, q_grad_w, o_grad_w = carried
        head_index, block_index, seq_start, row_start = item_info(item_index)
        queries = kept_queries[item_index]
        output = kept_outputs[item_index]
        log_total = kept_totals[item_index]
        grad_rows = lax.dynamic_slice(grad_attn_all, (row_start, 0), (QBLOCK, model_width))
        weight_o = lax.dynamic_slice(out_full, (head_index * HEAD_DIM, 0), (HEAD_DIM, model_width))
        grad_output = jnp.einsum(
            "td,hd->th", grad_rows, weight_o, preferred_element_type=jnp.float32
        ).astype(jnp.bfloat16)
        o_grad_w = add_window(
            o_grad_w,
            jnp.einsum("th,td->hd", output, grad_rows, preferred_element_type=jnp.float32),
            head_index * HEAD_DIM,
            0,
        )
        kv_head = head_index // group_size
        grad_queries, grad_keys, grad_values = lax.switch(
            block_index, backward_list, queries, grad_output, log_total, kv_all, seq_start, kv_head
        )
        cosine, sine_part = rotation(block_index * QBLOCK + jnp.arange(QBLOCK))
        grad_raw = rotate_back(grad_queries, cosine, sine_part).astype(jnp.bfloat16)
        rows_in = lax.dynamic_slice(normed_all, (row_start, 0), (QBLOCK, model_width))
        weight_q = lax.dynamic_slice(qkv_full, (0, head_index * HEAD_DIM), (model_width, HEAD_DIM))
        input_partial = add_window(
            input_partial,
            jnp.einsum("th,dh->td", grad_raw, weight_q, preferred_element_type=jnp.float32),
            row_start,
            0,
        )
        q_grad_w = add_window(
            q_grad_w,
            jnp.einsum("td,th->dh", rows_in, grad_raw, preferred_element_type=jnp.float32),
            0,
            head_index * HEAD_DIM,
        )
        kv_partial = add_window(kv_partial, grad_keys, seq_start, kv_head * HEAD_DIM)
        kv_partial = add_window(kv_partial, grad_values, seq_start, (KV_HEADS + kv_head) * HEAD_DIM)
        return ((input_partial, kv_partial, q_grad_w, o_grad_w), None)

    start_state = (
        jnp.zeros((group_rows, model_width), jnp.float32),
        jnp.zeros((group_rows, 2 * kv_width), jnp.float32),
        jnp.zeros((model_width, q_width), jnp.float32),
        jnp.zeros((q_width, model_width), jnp.float32),
    )
    (input_partial, kv_partial, q_grad_w, o_grad_w), unused = lax.scan(
        backward_item, start_state, jnp.arange(count_items)
    )
    input_sum, kv_sum = (
        lax.psum_scatter(input_partial, "mp", scatter_dimension=0, tiled=True),
        lax.psum_scatter(kv_partial, "mp", scatter_dimension=0, tiled=True),
    )
    cos_local, sin_local = rotation(local_pos)
    grad_keys_local = rotate_back(
        kv_sum[:, :kv_width].reshape(tok_dev, KV_HEADS, HEAD_DIM),
        cos_local[:, None, :],
        sin_local[:, None, :],
    )
    grad_kv = jnp.concatenate(
        [grad_keys_local.reshape(tok_dev, kv_width), kv_sum[:, kv_width:]], axis=1
    ).astype(jnp.bfloat16)
    grad_normed_one = input_sum + jnp.einsum(
        "tk,dk->td", grad_kv, weight_kv, preferred_element_type=jnp.float32
    )
    kv_grad_w = jnp.einsum("td,tk->dk", normed_one, grad_kv, preferred_element_type=jnp.float32)
    qkv_grad_full = jnp.concatenate([q_grad_w, kv_grad_w], axis=1)
    scaled_one = grad_normed_one * gain_one
    attn_gain_part = jnp.sum(grad_normed_one * residual * inverse_one, axis=0)
    input_grad = (
        grad_middle
        + inverse_one * scaled_one
        - residual * inverse_one**3 * jnp.mean(scaled_one * residual, axis=-1, keepdims=True)
    )
    qkv_grad, proj_grad, attn_gain_grad, ffn_gain_grad = (
        lax.psum_scatter(qkv_grad_full, ("rows", "mp"), scatter_dimension=0, tiled=True),
        lax.psum_scatter(o_grad_w, ("rows", "mp"), scatter_dimension=0, tiled=True),
        lax.psum_scatter(attn_gain_part, ("rows", "mp"), scatter_dimension=0, tiled=True),
        lax.psum_scatter(ffn_gain_part, ("rows", "mp"), scatter_dimension=0, tiled=True),
    )
    gate_grad, up_grad, down_grad = (
        lax.psum(gate_grad.astype(jnp.bfloat16), "rows").astype(jnp.float32),
        lax.psum(up_grad.astype(jnp.bfloat16), "rows").astype(jnp.float32),
        lax.psum(down_grad.astype(jnp.bfloat16), "rows").astype(jnp.float32),
    )
    return (
        outputs,
        input_grad,
        qkv_grad,
        proj_grad,
        gate_grad,
        up_grad,
        down_grad,
        attn_gain_grad,
        ffn_gain_grad,
    )


def solution(mesh):
    in_specs = (
        P(("rows", "mp"), None),
        P(("rows", "mp"), None),
        P("rows"),
        P(),
        P(("rows", "mp")),
        P(("rows", "mp"), None),
        P(("rows", "mp"), None),
        P(("rows", "mp")),
        P(None, "mp"),
        P(None, "mp"),
        P("mp", None),
    )
    out_specs = (
        P(("rows", "mp"), None),
        P(("rows", "mp"), None),
        P(("rows", "mp"), None),
        P(("rows", "mp"), None),
        P(None, "mp"),
        P(None, "mp"),
        P("mp", None),
        P(("rows", "mp")),
        P(("rows", "mp")),
    )
    return jax.shard_map(
        on_device, mesh=mesh, in_specs=in_specs, out_specs=out_specs, check_vma=False
    )
```

profile of v0, /device:TPU:0, one launch (start us, length us, event | category | flops | bytes accessed | tf_op | source)
XLA Modules:
  0.0 2238.0 jit_solution(10643275704402246868)
XLA Ops:
  10.4 43.2 %all-reduce.11 = (bf16[2048]{0:T(1024)(128)(2,1)S(1)}, bf16[2048]{0:T(1024)(128)(2,1)S(1)}) all-reduce(bf16[2048]{0:T(1024)(128)(2,1)S(1)} %dynamic-update-slice, bf16[2048]{0:T(1024)(128)(2,1)S(1)} %dynamic-update-slice.1), channel_id=1, replica_groups=mesh['rows'=4,'mp'=8] {'rows','mp'}, use_global_device_ids=true, to_apply=%add.6 | all-reduce | flops 4096 | bytes 16384
  59.7 29.9 %all-gather.10.cloned.1.call-done = bf16[2048,1920]{1,0:T(8,128)(2,1)} async-done(((bf16[64,1920]{1,0:T(8,128)(2,1)}), bf16[2048,1920]{1,0:T(8,128)(2,1)}) %all-gather.10.cloned.1.call-update) | async-done | bytes 7864336 | tf_op jit(solution)/shard_map/all_gather | solution.py:156
  97.7 58.8 %all-gather.14.cloned.1.call-done = bf16[1280,2048]{1,0:T(8,128)(2,1)} async-done(((bf16[40,2048]{1,0:T(8,128)(2,1)}), bf16[1280,2048]{1,0:T(8,128)(2,1)}) %all-gather.14.cloned.1.call-update) | async-done | bytes 5242896 | tf_op jit(solution)/shard_map/all_gather | solution.py:157
  156.5 82.6 %all-gather.8.cloned.1.call-done = bf16[2048,2048]{1,0:T(8,128)(2,1)} async-done(((bf16[256,2048]{1,0:T(8,128)(2,1)}), bf16[2048,2048]{1,0:T(8,128)(2,1)}) %all-gather.8.cloned.1.call-update) | async-done | bytes 8388624 | tf_op jit(solution)/shard_map/all_gather | solution.py:169
  239.1 34.5 %all-gather.12.cloned.1.call-done = bf16[2048,640]{1,0:T(8,128)(2,1)} async-done(((bf16[256,640]{1,0:T(8,128)(2,1)}), bf16[2048,640]{1,0:T(8,128)(2,1)}) %all-gather.12.cloned.1.call-update) | async-done | bytes 2621456 | tf_op jit(solution)/shard_map/all_gather | solution.py:170
  281.5 150.9 %while.42 = (s32[]{:T(128)}, f32[2048,2048]{1,0:T(8,128)}, bf16[10,512,64]{1,2,0:T(8,128)(2,1)}, bf16[10,512,64]{1,2,0:T(8,128)(2,1)}, f32[10,512]{1,0:T(8,128)S...) while((s32[]{:T(128)}, f32[2048,2048]{1,0:T(8,128)}, ...), condition=%wide.region_14.15_spmd, body=%wide.region_1.14_spmd.sunk | while | flops 547767360 | bytes 25982072 | solution.py:202
  432.5 169.8 %reduce-scatter.8.cloned.1.call-done = f32[256,2048]{1,0:T(8,128)} async-done(((f32[2048,2048]{1,0:T(8,128)}), f32[256,2048]{1,0:T(8,128)}) %reduce-scatter.8.cloned.1.call-update) | async-done | bytes 2097168 | tf_op jit(solution)/shard_map/reduce_scatter | solution.py:205
  607.7 9.9 psum.28
  622.9 64.7 %all-gather.16.cloned.1.call-done = bf16[2048,2048]{1,0:T(8,128)(2,1)} async-done(((bf16[256,2048]{1,0:T(8,128)(2,1)}), bf16[2048,2048]{1,0:T(8,128)(2,1)}) %all-gather.16.cloned.1.call-update) | async-done | bytes 8388624 | tf_op jit(solution)/shard_map/all_gather | solution.py:209
  687.6 11.8 fusion.167
  699.4 8.5 fusion.166
  707.9 62.5 %all-gather.18.cloned.1.call-done = bf16[2048,2048]{1,0:T(8,128)(2,1)} async-done(((bf16[256,2048]{1,0:T(8,128)(2,1)}), bf16[2048,2048]{1,0:T(8,128)(2,1)}) %all-gather.18.cloned.1.call-update) | async-done | bytes 8388624 | tf_op jit(solution)/shard_map/all_gather | solution.py:225
  770.4 15.7 multiply_convert_fusion.2
  786.1 13.3 fusion.168
  799.4 14.1 convolution_add_fusion.2
  813.6 10.8 convolution_convert_fusion
  824.5 156.0 %reduce-scatter.12.cloned.1.call-done = f32[256,2048]{1,0:T(8,128)} async-done(((f32[2048,2048]{1,0:T(8,128)}), f32[256,2048]{1,0:T(8,128)}) %reduce-scatter.12.cloned.1.call-update) | async-done | bytes 2097168 | tf_op jit(solution)/shard_map/reduce_scatter | solution.py:241
  983.3 87.6 %reduce-scatter.10.cloned.1.call-done = bf16[256,2048]{1,0:T(8,128)(2,1)} async-done(((bf16[2048,2048]{1,0:T(8,128)(2,1)}), bf16[256,2048]{1,0:T(8,128)(2,1)}) %reduce-scatter.10.cloned.1.call-update) | async-done | bytes 1048592 | tf_op jit(solution)/shard_map/reduce_scatter | solution.py:214
  1077.9 78.2 %all-gather.20.cloned.1.call-done = bf16[2048,2048]{1,0:T(8,128)(2,1)} async-done(((bf16[256,2048]{1,0:T(8,128)(2,1)}), bf16[2048,2048]{1,0:T(8,128)(2,1)}) %all-gather.20.cloned.1.call-update) | async-done | bytes 8388624 | tf_op jit(solution)/shard_map/all_gather | solution.py:249
  1177.5 293.2 %while.43 = (s32[]{:T(128)}, f32[2048,2048]{1,0:T(8,128)}, f32[2048,640]{0,1:T(8,128)}, f32[2048,1280]{0,1:T(8,128)}, f32[1280,2048]{1,0:T(8,128)}, /*index=5*/s...) while((s32[]{:T(128)}, f32[2048,2048]{1,0:T(8,128)}, ...), condition=%wide.region_32.33_spmd, body=%wide.region_23.32_spmd.sunk | while | flops 1220625536 | bytes 55792484 | solution.py:298
  1239.8 9.2 conditional.18
  1270.0 10.5 conditional.18
  1357.9 9.2 conditional.18
  1388.1 10.5 conditional.18
  1470.7 12.2 convolution_convert_fusion.1
  1501.3 11.6 copy.61
  1512.9 21.2 reduce-scatter.16.cloned.1.call-done
  1546.4 180.2 %all-reduce.15.cloned.1.call-done = (bf16[2048,768]{1,0:T(8,128)(2,1)}, bf16[2048,768]{1,0:T(8,128)(2,1)}, bf16[768,2048]{1,0:T(8,128)(2,1)}) async-done(((bf16[2048,768]{1,0:T(8,128)(2,1)}, bf16[2048,768]{1,0:T(8,128)(2,1)}, bf16[768,2048]{1,0:T(8,128)(2,1)}), (bf16[2048,768]{1,0:T(8,128)(2,1)}, bf16[2048,768]{1,0:T(8,128)(2,1)}, bf16[768,2048]{1,0:T(8,128)(2,1)})) %all-reduce.15.cloned.1.call-update) | async-done | bytes 9437200 | tf_op jit(solution)/shard_map/psum | solution.py:333
  1739.3 158.0 %reduce-scatter.14.cloned.1.call-done = f32[256,2048]{1,0:T(8,128)} async-done(((f32[2048,2048]{1,0:T(8,128)}), f32[256,2048]{1,0:T(8,128)}) %reduce-scatter.14.cloned.1.call-update) | async-done | bytes 2097168 | tf_op jit(solution)/shard_map/reduce_scatter | solution.py:302
  1902.3 38.8 %all-reduce.10 = (f32[2048]{0:T(1024)S(1)}, f32[2048]{0:T(1024)S(1)}) all-reduce(f32[2048]{0:T(1024)S(1)} %get-tuple-element.1396, f32[2048]{0:T(1024)S(1)} %copy-done.14), channel_id=9, replica_groups=mesh['rows'=4,'mp'=8] {'rows','mp'}, use_global_device_ids=true, to_apply=%region_42.43.clone | all-reduce | flops 4096 | bytes 32768
  1947.0 109.4 %reduce-scatter.20.cloned.1.call-done = f32[40,2048]{1,0:T(8,128)} async-done(((f32[1280,2048]{1,0:T(8,128)}), f32[40,2048]{1,0:T(8,128)}) %reduce-scatter.20.cloned.1.call-update) | async-done | bytes 327696 | tf_op jit(solution)/shard_map/reduce_scatter | solution.py:328
  2056.3 174.8 %reduce-scatter.18.cloned.1.call-done = f32[64,1920]{1,0:T(8,128)} async-done(((f32[2048,1920]{1,0:T(8,128)}), f32[64,1920]{1,0:T(8,128)}) %reduce-scatter.18.cloned.1.call-update) | async-done | bytes 491536 | tf_op jit(solution)/shard_map/reduce_scatter | solution.py:327
  (498 shorter events, 621.9 us)
Async XLA Ops:
  7.2 763.2 %copy-start = (bf16[768,2048]{1,0:T(8,128)(2,1)S(1)}, bf16[768,2048]{1,0:T(8,128)(2,1)}, u32[]{:S(2)}) copy-start(bf16[768,2048]{1,0:T(8,128)(2,1)} %param.33) | copy-start | bytes 9437188
  7.2 82.5 %all-gather.10.cloned.1.call-start = ((), (), s32[]{:S(2)}) async-start(), calls=%async_computation.8 | async-start | bytes 8110080 | tf_op jit(solution)/shard_map/all_gather | solution.py:156
  7.9 148.6 %all-gather.14.cloned.1.call-start = ((), (), s32[]{:S(2)}) async-start(), calls=%async_computation.10 | async-start | bytes 5406720 | tf_op jit(solution)/shard_map/all_gather | solution.py:157
  8.7 230.4 %all-gather.8.cloned.1.call-start = ((), (), s32[]{:S(2)}) async-start(), calls=%async_computation.7 | async-start | bytes 9437184 | tf_op jit(solution)/shard_map/all_gather | solution.py:169
  58.8 214.7 %all-gather.12.cloned.1.call-start = ((), (), s32[]{:S(2)}) async-start(), calls=%async_computation.9 | async-start | bytes 2949120 | tf_op jit(solution)/shard_map/all_gather | solution.py:170
  97.4 504.8 %reduce-scatter.8.cloned.1.call-start = ((), (), s32[]{:S(2)}) async-start(), calls=%async_computation.11 | async-start | bytes 18874368 | tf_op jit(solution)/shard_map/reduce_scatter | solution.py:205
  432.4 255.2 %all-gather.16.cloned.1.call-start = ((), (), s32[]{:S(2)}) async-start(), calls=%async_computation.12 | async-start | bytes 9437184 | tf_op jit(solution)/shard_map/all_gather | solution.py:209
  604.5 13.1 copy-start.23
  607.0 163.4 %all-gather.18.cloned.1.call-start = ((), (), s32[]{:S(2)}) async-start(), calls=%async_computation.14 | async-start | bytes 9437184 | tf_op jit(solution)/shard_map/all_gather | solution.py:225
  622.7 357.9 %reduce-scatter.12.cloned.1.call-start = ((), (), s32[]{:S(2)}) async-start(), calls=%async_computation.15 | async-start | bytes 18874368 | tf_op jit(solution)/shard_map/reduce_scatter | solution.py:241
  770.4 15.7 copy-start.21
  786.1 13.3 copy-start.24
  786.1 13.3 copy-start.22
  813.6 257.2 %reduce-scatter.10.cloned.1.call-start = ((), (), s32[]{:S(2)}) async-start(), calls=%async_computation.13 | async-start | bytes 9437184 | tf_op jit(solution)/shard_map/reduce_scatter | solution.py:214
  824.4 156.1 %copy-start.4 = (f32[256,2048]{1,0:T(8,128)S(1)}, f32[256,2048]{1,0:T(8,128)}, u32[]{:S(2)}) copy-start(f32[256,2048]{1,0:T(8,128)} %copy-done.3) | copy-start | bytes 6291460
  824.5 246.3 %copy-start.7 = (bf16[256,2048]{1,0:T(8,128)(2,1)S(1)}, bf16[256,2048]{1,0:T(8,128)(2,1)}, u32[]{:S(2)}) copy-start(bf16[256,2048]{1,0:T(8,128)(2,1)} %param.24) | copy-start | bytes 3145732
  824.5 331.6 %all-gather.20.cloned.1.call-start = ((), (), s32[]{:S(2)}) async-start(), calls=%async_computation.16 | async-start | bytes 9437184 | tf_op jit(solution)/shard_map/all_gather | solution.py:249
  1075.5 458.6 %reduce-scatter.16.cloned.1.call-start = ((), (), s32[]{:S(2)}) async-start(), calls=%async_computation.18 | async-start | bytes 5898240 | tf_op jit(solution)/shard_map/reduce_scatter | solution.py:303
  1470.7 12.2 copy-start.25
  1470.7 255.9 %all-reduce.15.cloned.1.call-start = ((), (), s32[]{:S(2)}) async-start(), calls=%async_computation.21 | async-start | bytes 18874368 | tf_op jit(solution)/shard_map/psum | solution.py:333
  1499.9 397.3 %reduce-scatter.14.cloned.1.call-start = ((), (), s32[]{:S(2)}) async-start(), calls=%async_computation.17 | async-start | bytes 18874368 | tf_op jit(solution)/shard_map/reduce_scatter | solution.py:302
  1500.7 555.7 %reduce-scatter.20.cloned.1.call-start = ((), (), s32[]{:S(2)}) async-start(), calls=%async_computation.20 | async-start | bytes 10813440 | tf_op jit(solution)/shard_map/reduce_scatter | solution.py:328
  1501.2 729.9 %reduce-scatter.18.cloned.1.call-start = ((), (), s32[]{:S(2)}) async-start(), calls=%async_computation.19 | async-start | bytes 16220160 | tf_op jit(solution)/shard_map/reduce_scatter | solution.py:327
  1501.3 34.8 %copy-start.10 = (f32[256,32]{0,1:T(8,128)S(1)}, f32[256,32]{0,1:T(8,128)}, u32[]{:S(2)}) copy-start(f32[256,32]{0,1:T(8,128)} %get-tuple-element.1491) | copy-start | bytes 98308
  1501.3 34.8 %copy-start.11 = (f32[256,32]{0,1:T(8,128)S(1)}, f32[256,32]{0,1:T(8,128)}, u32[]{:S(2)}) copy-start(f32[256,32]{0,1:T(8,128)} %get-tuple-element.1492) | copy-start | bytes 98308
  1501.3 34.9 %copy-start.6 = (bf16[256,2048]{1,0:T(8,128)(2,1)S(1)}, bf16[256,2048]{1,0:T(8,128)(2,1)}, u32[]{:S(2)}) copy-start(bf16[256,2048]{1,0:T(8,128)(2,1)} %fusion.148) | copy-start | bytes 3145732
  1735.7 161.5 %copy-start.5 = (bf16[256,2048]{1,0:T(8,128)(2,1)S(1)}, bf16[256,2048]{1,0:T(8,128)(2,1)}, u32[]{:S(2)}) copy-start(bf16[256,2048]{1,0:T(8,128)(2,1)} %param.23) | copy-start | bytes 3145732
  1735.7 161.5 %copy-start.13 = (f32[2048]{0:T(1024)S(1)}, f32[2048]{0:T(1024)}, u32[]{:S(2)}) copy-start(f32[2048]{0:T(1024)} %copy-done.12) | copy-start | bytes 24580
  1735.7 161.5 %copy-start.16 = (f32[256]{0:T(256)S(1)}, f32[256]{0:T(256)}, u32[]{:S(2)}) copy-start(f32[256]{0:T(256)} %copy-done.15) | copy-start | bytes 3076
  1739.2 163.1 %copy-start.14 = (f32[2048]{0:T(1024)S(1)}, f32[2048]{0:T(1024)}, u32[]{:S(2)}) copy-start(f32[2048]{0:T(1024)} %get-tuple-element.1394) | copy-start | bytes 24580
  1739.3 203.1 %copy-start.17 = (f32[256]{0:T(256)S(1)}, f32[256]{0:T(256)}, u32[]{:S(2)}) copy-start(f32[256]{0:T(256)} %get-tuple-element.1493) | copy-start | bytes 3076
  1942.3 288.8 %copy-start.1 = (bf16[768,2048]{1,0:T(8,128)(2,1)S(1)}, bf16[768,2048]{1,0:T(8,128)(2,1)}, u32[]{:S(2)}) copy-start(bf16[768,2048]{1,0:T(8,128)(2,1)} %param.33) | copy-start | bytes 9437188
  (10 other events, 61.3 us)
Sparse Core Ops, SparseCore 0:
  11.0 78.5 all-gather.9
  92.5 63.9 all-gather.13
  158.1 80.9 all-gather.7
  241.1 32.3 all-gather.11
  432.5 169.6 reduce-scatter.7
  607.1 80.4 all-gather.15
  689.8 80.5 all-gather.17
  813.7 166.7 reduce-scatter.11
  982.8 87.9 reduce-scatter.9
  1075.6 80.4 all-gather.19
  1470.8 63.3 reduce-scatter.15
  1538.4 188.0 all-reduce.14
  1728.9 168.2 reduce-scatter.13
  1899.9 156.3 reduce-scatter.19
  2062.8 168.3 reduce-scatter.17
where the time goes:
time: 2250 us; the launch traced here: 2240 us
  waiting for transfers between devices  1470 us (65%)
  matrix products  430 us (19%)
  other arithmetic  110 us (5%)
  blocking collectives  91.9 us (4%)
  local copies, waits for them, and re-layouts  82.2 us (4%)
  loops' own time  36 us (2%)
    psum x1, waiting for transfers between devices, on_device(): lax.psum(gate_grad.astype(jnp.bfloat16), 'rows').astype(jnp.float32)  180 us
    reduce_scatter x1, waiting for transfers between devices, on_device(): lax.psum_scatter(qkv_grad_full, ('rows', 'mp'), scatter_dimension=0, tile...  175 us
    reduce_scatter x1, waiting for transfers between devices, on_device(): lax.psum_scatter(attn_partial, 'mp', scatter_dimension=0, tiled=True)  170 us
    reduce_scatter x1, waiting for transfers between devices, on_device(): lax.psum_scatter(input_partial, 'mp', scatter_dimension=0, tiled=True)  158 us
    reduce_scatter x1, waiting for transfers between devices, on_device(): lax.psum_scatter(mid_partial, 'mp', scatter_dimension=0, tiled=True)  156 us
    reduce_scatter x1, waiting for transfers between devices, on_device(): lax.psum_scatter(o_grad_w, ('rows', 'mp'), scatter_dimension=0, tiled=True)  109 us
    reduce_scatter x1, waiting for transfers between devices, on_device(): lax.psum_scatter(ffn_part.astype(jnp.bfloat16), 'mp', scatter_dimension=0...  87.6 us
    all_gather x1, waiting for transfers between devices, on_device(): lax.all_gather(normed_one, 'mp', axis=0, tiled=True)  82.6 us
  transfers between devices with their start and end apart: 15, of which 15 were waited for; matrix products, arithmetic and copies ran while one was open for 6% of the time, Pallas kernels for 0%

commit v1 on v0

--- a/solution.py
+++ b/solution.py
@@ -330,7 +330,9 @@
         lax.psum_scatter(ffn_gain_part, ("rows", "mp"), scatter_dimension=0, tiled=True),
     )
     gate_grad, up_grad, down_grad = (
-        lax.psum(gate_grad.astype(jnp.bfloat16), "rows").astype(jnp.float32),
+        jnp.sum(lax.all_gather(gate_grad.astype(jnp.bfloat16), axis_name="rows"), axis=0).astype(
+            jnp.float32
+        ),
         lax.psum(up_grad.astype(jnp.bfloat16), "rows").astype(jnp.float32),
         lax.psum(down_grad.astype(jnp.bfloat16), "rows").astype(jnp.float32),
     )

time: 2250 us -> 2320 us (1.031)
  waiting for transfers between devices: 1470 us -> 1530 us
    all_gather x0 -> x1, waiting for transfers between devices: none -> 116 us  [on_device(): lax.all_gather(gate_grad.astype(jnp.bfloat16), axis_name='rows')]
    psum x1, waiting for transfers between devices: 180 us -> 129 us  [on_device(): lax.psum(up_grad.astype(jnp.bfloat16), 'rows').astype(jnp.float32)]
  transfers between devices with their start and end apart: 15 -> 16, of which waited for: 15 -> 16; matrix products, arithmetic and copies ran while one was open for 6% -> 6% of each run, Pallas kernels for 0% -> 0%
where the time goes in v1:
time: 2320 us; the launch traced here: 2310 us
  waiting for transfers between devices  1530 us (66%)
  matrix products  431 us (19%)
  other arithmetic  120 us (5%)
  blocking collectives  92.3 us (4%)
  local copies, waits for them, and re-layouts  84.3 us (4%)
  loops' own time  36 us (2%)
    reduce_scatter x1, waiting for transfers between devices, on_device(): lax.psum_scatter(qkv_grad_full, ('rows', 'mp'), scatter_dimension=0, tile...  175 us
    reduce_scatter x1, waiting for transfers between devices, on_device(): lax.psum_scatter(attn_partial, 'mp', scatter_dimension=0, tiled=True)  170 us
    reduce_scatter x1, waiting for transfers between devices, on_device(): lax.psum_scatter(input_partial, 'mp', scatter_dimension=0, tiled=True)  156 us
    reduce_scatter x1, waiting for transfers between devices, on_device(): lax.psum_scatter(mid_partial, 'mp', scatter_dimension=0, tiled=True)  156 us
    psum x1, waiting for transfers between devices, on_device(): lax.psum(up_grad.astype(jnp.bfloat16), 'rows').astype(jnp.float32)  129 us
    all_gather x1, waiting for transfers between devices, on_device(): lax.all_gather(gate_grad.astype(jnp.bfloat16), axis_name='rows')  116 us
    reduce_scatter x1, waiting for transfers between devices, on_device(): lax.psum_scatter(o_grad_w, ('rows', 'mp'), scatter_dimension=0, tiled=True)  109 us
    reduce_scatter x1, waiting for transfers between devices, on_device(): lax.psum_scatter(ffn_part.astype(jnp.bfloat16), 'mp', scatter_dimension=0...  87.5 us
  transfers between devices with their start and end apart: 16, of which 16 were waited for; matrix products, arithmetic and copies ran while one was open for 6% of the time, Pallas kernels for 0%

profile of v1, /device:TPU:0, one launch (start us, length us, event | category | flops | bytes accessed | tf_op | source)
XLA Modules:
  0.0 2311.9 jit_solution(7410365720003434355)
XLA Ops:
  10.4 43.2 %all-reduce.11 = (bf16[2048]{0:T(1024)(128)(2,1)S(1)}, bf16[2048]{0:T(1024)(128)(2,1)S(1)}) all-reduce(bf16[2048]{0:T(1024)(128)(2,1)S(1)} %dynamic-update-slice, bf16[2048]{0:T(1024)(128)(2,1)S(1)} %dynamic-update-slice.1), channel_id=1, replica_groups=mesh['rows'=4,'mp'=8] {'rows','mp'}, use_global_device_ids=true, to_apply=%add.6 | all-reduce | flops 4096 | bytes 16384
  59.8 29.9 %all-gather.12.cloned.1.call-done = bf16[2048,1920]{1,0:T(8,128)(2,1)} async-done(((bf16[64,1920]{1,0:T(8,128)(2,1)}), bf16[2048,1920]{1,0:T(8,128)(2,1)}) %all-gather.12.cloned.1.call-update) | async-done | bytes 7864336 | tf_op jit(solution)/shard_map/all_gather | solution.py:156
  97.7 58.8 %all-gather.16.cloned.1.call-done = bf16[1280,2048]{1,0:T(8,128)(2,1)} async-done(((bf16[40,2048]{1,0:T(8,128)(2,1)}), bf16[1280,2048]{1,0:T(8,128)(2,1)}) %all-gather.16.cloned.1.call-update) | async-done | bytes 5242896 | tf_op jit(solution)/shard_map/all_gather | solution.py:157
  156.5 82.6 %all-gather.10.cloned.1.call-done = bf16[2048,2048]{1,0:T(8,128)(2,1)} async-done(((bf16[256,2048]{1,0:T(8,128)(2,1)}), bf16[2048,2048]{1,0:T(8,128)(2,1)}) %all-gather.10.cloned.1.call-update) | async-done | bytes 8388624 | tf_op jit(solution)/shard_map/all_gather | solution.py:169
  239.1 34.5 %all-gather.14.cloned.1.call-done = bf16[2048,640]{1,0:T(8,128)(2,1)} async-done(((bf16[256,640]{1,0:T(8,128)(2,1)}), bf16[2048,640]{1,0:T(8,128)(2,1)}) %all-gather.14.cloned.1.call-update) | async-done | bytes 2621456 | tf_op jit(solution)/shard_map/all_gather | solution.py:170
  281.4 150.8 %while.42 = (s32[]{:T(128)}, f32[2048,2048]{1,0:T(8,128)}, bf16[10,512,64]{1,2,0:T(8,128)(2,1)}, bf16[10,512,64]{1,2,0:T(8,128)(2,1)}, f32[10,512]{1,0:T(8,128)S...) while((s32[]{:T(128)}, f32[2048,2048]{1,0:T(8,128)}, ...), condition=%wide.region_14.15_spmd, body=%wide.region_1.14_spmd.sunk | while | flops 547767360 | bytes 25982072 | solution.py:202
  432.3 169.8 %reduce-scatter.8.cloned.1.call-done = f32[256,2048]{1,0:T(8,128)} async-done(((f32[2048,2048]{1,0:T(8,128)}), f32[256,2048]{1,0:T(8,128)}) %reduce-scatter.8.cloned.1.call-update) | async-done | bytes 2097168 | tf_op jit(solution)/shard_map/reduce_scatter | solution.py:205
  607.6 9.9 psum.21
  622.8 64.6 %all-gather.18.cloned.1.call-done = bf16[2048,2048]{1,0:T(8,128)(2,1)} async-done(((bf16[256,2048]{1,0:T(8,128)(2,1)}), bf16[2048,2048]{1,0:T(8,128)(2,1)}) %all-gather.18.cloned.1.call-update) | async-done | bytes 8388624 | tf_op jit(solution)/shard_map/all_gather | solution.py:209
  687.5 11.8 fusion.167
  707.8 62.5 %all-gather.20.cloned.1.call-done = bf16[2048,2048]{1,0:T(8,128)(2,1)} async-done(((bf16[256,2048]{1,0:T(8,128)(2,1)}), bf16[2048,2048]{1,0:T(8,128)(2,1)}) %all-gather.20.cloned.1.call-update) | async-done | bytes 8388624 | tf_op jit(solution)/shard_map/all_gather | solution.py:225
  770.3 15.7 multiply_convert_fusion.2
  786.0 13.2 fusion.168
  799.2 14.1 convolution_add_fusion.2
  813.3 10.9 convolution_convert_fusion
  824.3 155.9 %reduce-scatter.12.cloned.1.call-done = f32[256,2048]{1,0:T(8,128)} async-done(((f32[2048,2048]{1,0:T(8,128)}), f32[256,2048]{1,0:T(8,128)}) %reduce-scatter.12.cloned.1.call-update) | async-done | bytes 2097168 | tf_op jit(solution)/shard_map/reduce_scatter | solution.py:241
  982.9 87.5 %reduce-scatter.10.cloned.1.call-done = bf16[256,2048]{1,0:T(8,128)(2,1)} async-done(((bf16[2048,2048]{1,0:T(8,128)(2,1)}), bf16[256,2048]{1,0:T(8,128)(2,1)}) %reduce-scatter.10.cloned.1.call-update) | async-done | bytes 1048592 | tf_op jit(solution)/shard_map/reduce_scatter | solution.py:214
  1077.6 78.1 %all-gather.22.cloned.1.call-done = bf16[2048,2048]{1,0:T(8,128)(2,1)} async-done(((bf16[256,2048]{1,0:T(8,128)(2,1)}), bf16[2048,2048]{1,0:T(8,128)(2,1)}) %all-gather.22.cloned.1.call-update) | async-done | bytes 8388624 | tf_op jit(solution)/shard_map/all_gather | solution.py:249
  1177.2 293.0 %while.43 = (s32[]{:T(128)}, f32[2048,2048]{1,0:T(8,128)}, f32[2048,640]{0,1:T(8,128)}, f32[2048,1280]{0,1:T(8,128)}, f32[1280,2048]{1,0:T(8,128)}, /*index=5*/s...) while((s32[]{:T(128)}, f32[2048,2048]{1,0:T(8,128)}, ...), condition=%wide.region_32.33_spmd, body=%wide.region_23.32_spmd.sunk | while | flops 1220625536 | bytes 55792484 | solution.py:298
  1269.7 10.5 conditional.18
  1357.5 9.2 conditional.18
  1387.7 10.5 conditional.18
  1470.3 12.1 convolution_convert_fusion.1
  1492.8 10.5 convolution_convert_fusion.3
  1504.6 11.6 copy.61
  1516.2 18.3 reduce-scatter.16.cloned.1.call-done
  1546.7 128.8 %all-reduce.15.cloned.1.call-done = (bf16[2048,768]{1,0:T(8,128)(2,1)}, bf16[768,2048]{1,0:T(8,128)(2,1)}) async-done(((bf16[2048,768]{1,0:T(8,128)(2,1)}, bf16[768,2048]{1,0:T(8,128)(2,1)}), (bf16[2048,768]{1,0:T(8,128)(2,1)}, bf16[768,2048]{1,0:T(8,128)(2,1)})) %all-reduce.15.cloned.1.call-update) | async-done | bytes 6291472 | tf_op jit(solution)/shard_map/psum | solution.py:336
  1684.4 116.2 %all-gather.24.cloned.1.call-done = bf16[8192,768]{1,0:T(8,128)(2,1)} async-done(((bf16[2048,768]{1,0:T(8,128)(2,1)}), bf16[8192,768]{1,0:T(8,128)(2,1)}) %all-gather.24.cloned.1.call-update) | async-done | bytes 12582928 | tf_op jit(solution)/shard_map/all_gather | solution.py:333
  1814.8 156.2 %reduce-scatter.14.cloned.1.call-done = f32[256,2048]{1,0:T(8,128)} async-done(((f32[2048,2048]{1,0:T(8,128)}), f32[256,2048]{1,0:T(8,128)}) %reduce-scatter.14.cloned.1.call-update) | async-done | bytes 2097168 | tf_op jit(solution)/shard_map/reduce_scatter | solution.py:302
  1976.2 39.2 %all-reduce.10 = (f32[2048]{0:T(1024)S(1)}, f32[2048]{0:T(1024)S(1)}) all-reduce(f32[2048]{0:T(1024)S(1)} %get-tuple-element.1396, f32[2048]{0:T(1024)S(1)} %copy-done.13), channel_id=10, replica_groups=mesh['rows'=4,'mp'=8] {'rows','mp'}, use_global_device_ids=true, to_apply=%region_42.43.clone | all-reduce | flops 4096 | bytes 32768
  2021.2 109.0 %reduce-scatter.20.cloned.1.call-done = f32[40,2048]{1,0:T(8,128)} async-done(((f32[1280,2048]{1,0:T(8,128)}), f32[40,2048]{1,0:T(8,128)}) %reduce-scatter.20.cloned.1.call-update) | async-done | bytes 327696 | tf_op jit(solution)/shard_map/reduce_scatter | solution.py:328
  2130.2 174.7 %reduce-scatter.18.cloned.1.call-done = f32[64,1920]{1,0:T(8,128)} async-done(((f32[2048,1920]{1,0:T(8,128)}), f32[64,1920]{1,0:T(8,128)}) %reduce-scatter.18.cloned.1.call-update) | async-done | bytes 491536 | tf_op jit(solution)/shard_map/reduce_scatter | solution.py:327
  (500 shorter events, 643.2 us)
Async XLA Ops:
  7.2 763.1 %copy-start = (bf16[768,2048]{1,0:T(8,128)(2,1)S(1)}, bf16[768,2048]{1,0:T(8,128)(2,1)}, u32[]{:S(2)}) copy-start(bf16[768,2048]{1,0:T(8,128)(2,1)} %param.33) | copy-start | bytes 9437188
  7.2 82.4 %all-gather.12.cloned.1.call-start = ((), (), s32[]{:S(2)}) async-start(), calls=%async_computation.8 | async-start | bytes 8110080 | tf_op jit(solution)/shard_map/all_gather | solution.py:156
  7.9 148.6 %all-gather.16.cloned.1.call-start = ((), (), s32[]{:S(2)}) async-start(), calls=%async_computation.10 | async-start | bytes 5406720 | tf_op jit(solution)/shard_map/all_gather | solution.py:157
  8.7 230.4 %all-gather.10.cloned.1.call-start = ((), (), s32[]{:S(2)}) async-start(), calls=%async_computation.7 | async-start | bytes 9437184 | tf_op jit(solution)/shard_map/all_gather | solution.py:169
  58.9 214.7 %all-gather.14.cloned.1.call-start = ((), (), s32[]{:S(2)}) async-start(), calls=%async_computation.9 | async-start | bytes 2949120 | tf_op jit(solution)/shard_map/all_gather | solution.py:170
  97.4 504.7 %reduce-scatter.8.cloned.1.call-start = ((), (), s32[]{:S(2)}) async-start(), calls=%async_computation.11 | async-start | bytes 18874368 | tf_op jit(solution)/shard_map/reduce_scatter | solution.py:205
  432.2 255.2 %all-gather.18.cloned.1.call-start = ((), (), s32[]{:S(2)}) async-start(), calls=%async_computation.12 | async-start | bytes 9437184 | tf_op jit(solution)/shard_map/all_gather | solution.py:209
  604.3 13.1 copy-start.22
  606.9 163.4 %all-gather.20.cloned.1.call-start = ((), (), s32[]{:S(2)}) async-start(), calls=%async_computation.14 | async-start | bytes 9437184 | tf_op jit(solution)/shard_map/all_gather | solution.py:225
  622.5 357.7 %reduce-scatter.12.cloned.1.call-start = ((), (), s32[]{:S(2)}) async-start(), calls=%async_computation.15 | async-start | bytes 18874368 | tf_op jit(solution)/shard_map/reduce_scatter | solution.py:241
  770.3 15.7 copy-start.20
  786.0 13.2 copy-start.23
  786.0 13.2 copy-start.21
  813.3 257.2 %reduce-scatter.10.cloned.1.call-start = ((), (), s32[]{:S(2)}) async-start(), calls=%async_computation.13 | async-start | bytes 9437184 | tf_op jit(solution)/shard_map/reduce_scatter | solution.py:214
  824.2 156.0 %copy-start.4 = (f32[256,2048]{1,0:T(8,128)S(1)}, f32[256,2048]{1,0:T(8,128)}, u32[]{:S(2)}) copy-start(f32[256,2048]{1,0:T(8,128)} %copy-done.3) | copy-start | bytes 6291460
  824.3 246.2 %copy-start.7 = (bf16[256,2048]{1,0:T(8,128)(2,1)S(1)}, bf16[256,2048]{1,0:T(8,128)(2,1)}, u32[]{:S(2)}) copy-start(bf16[256,2048]{1,0:T(8,128)(2,1)} %param.24) | copy-start | bytes 3145732
  824.3 331.5 %all-gather.22.cloned.1.call-start = ((), (), s32[]{:S(2)}) async-start(), calls=%async_computation.16 | async-start | bytes 9437184 | tf_op jit(solution)/shard_map/all_gather | solution.py:249
  1075.2 459.3 %reduce-scatter.16.cloned.1.call-start = ((), (), s32[]{:S(2)}) async-start(), calls=%async_computation.18 | async-start | bytes 5898240 | tf_op jit(solution)/shard_map/reduce_scatter | solution.py:303
  1470.3 205.3 %all-reduce.15.cloned.1.call-start = ((), (), s32[]{:S(2)}) async-start(), calls=%async_computation.22 | async-start | bytes 12582912 | tf_op jit(solution)/shard_map/psum | solution.py:336
  1490.9 309.6 %all-gather.24.cloned.1.call-start = ((), (), s32[]{:S(2)}) async-start(), calls=%async_computation.21 | async-start | bytes 15728640 | tf_op jit(solution)/shard_map/all_gather | solution.py:333
  1503.3 467.7 %reduce-scatter.14.cloned.1.call-start = ((), (), s32[]{:S(2)}) async-start(), calls=%async_computation.17 | async-start | bytes 18874368 | tf_op jit(solution)/shard_map/reduce_scatter | solution.py:302
  1503.9 626.3 %reduce-scatter.20.cloned.1.call-start = ((), (), s32[]{:S(2)}) async-start(), calls=%async_computation.20 | async-start | bytes 10813440 | tf_op jit(solution)/shard_map/reduce_scatter | solution.py:328
  1504.5 800.5 %reduce-scatter.18.cloned.1.call-start = ((), (), s32[]{:S(2)}) async-start(), calls=%async_computation.19 | async-start | bytes 16220160 | tf_op jit(solution)/shard_map/reduce_scatter | solution.py:327
  1504.5 31.9 %copy-start.9 = (f32[256,32]{0,1:T(8,128)S(1)}, f32[256,32]{0,1:T(8,128)}, u32[]{:S(2)}) copy-start(f32[256,32]{0,1:T(8,128)} %get-tuple-element.1490) | copy-start | bytes 98308
  1504.5 31.9 %copy-start.10 = (f32[256,32]{0,1:T(8,128)S(1)}, f32[256,32]{0,1:T(8,128)}, u32[]{:S(2)}) copy-start(f32[256,32]{0,1:T(8,128)} %get-tuple-element.1491) | copy-start | bytes 98308
  1504.5 32.0 %copy-start.6 = (bf16[256,2048]{1,0:T(8,128)(2,1)S(1)}, bf16[256,2048]{1,0:T(8,128)(2,1)}, u32[]{:S(2)}) copy-start(bf16[256,2048]{1,0:T(8,128)(2,1)} %fusion.148) | copy-start | bytes 3145732
  1809.6 161.4 %copy-start.5 = (bf16[256,2048]{1,0:T(8,128)(2,1)S(1)}, bf16[256,2048]{1,0:T(8,128)(2,1)}, u32[]{:S(2)}) copy-start(bf16[256,2048]{1,0:T(8,128)(2,1)} %param.23) | copy-start | bytes 3145732
  1809.6 161.4 %copy-start.12 = (f32[2048]{0:T(1024)S(1)}, f32[2048]{0:T(1024)}, u32[]{:S(2)}) copy-start(f32[2048]{0:T(1024)} %copy-done.11) | copy-start | bytes 24580
  1809.6 161.4 %copy-start.15 = (f32[256]{0:T(256)S(1)}, f32[256]{0:T(256)}, u32[]{:S(2)}) copy-start(f32[256]{0:T(256)} %copy-done.14) | copy-start | bytes 3076
  1814.8 161.4 %copy-start.13 = (f32[2048]{0:T(1024)S(1)}, f32[2048]{0:T(1024)}, u32[]{:S(2)}) copy-start(f32[2048]{0:T(1024)} %get-tuple-element.1394) | copy-start | bytes 24580
  1814.8 201.8 %copy-start.16 = (f32[256]{0:T(256)S(1)}, f32[256]{0:T(256)}, u32[]{:S(2)}) copy-start(f32[256]{0:T(256)} %get-tuple-element.1492) | copy-start | bytes 3076
  2016.5 288.4 %copy-start.1 = (bf16[768,2048]{1,0:T(8,128)(2,1)S(1)}, bf16[768,2048]{1,0:T(8,128)(2,1)}, u32[]{:S(2)}) copy-start(bf16[768,2048]{1,0:T(8,128)(2,1)} %param.33) | copy-start | bytes 9437188
  (10 other events, 63.0 us)
Sparse Core Ops, SparseCore 0:
  11.0 78.5 all-gather.11
  92.5 63.9 all-gather.15
  158.1 80.9 all-gather.9
  241.1 32.3 all-gather.13
  432.4 169.7 reduce-scatter.7
  607.0 80.4 all-gather.17
  689.6 80.5 all-gather.19
  813.4 166.7 reduce-scatter.11
  982.5 87.9 reduce-scatter.9
  1075.3 80.3 all-gather.21
  1470.4 64.0 reduce-scatter.15
  1538.4 137.1 all-reduce.14
  1678.0 122.5 all-gather.23
  1802.7 168.2 reduce-scatter.13
  1973.7 156.3 reduce-scatter.19
  2136.6 168.2 reduce-scatter.17
